TPU v7x, 128 devices: a whole 4x4x4 slice. The times are simulated.
128 devices in a mesh: seq: 8 (over y, core), nbr: 16 (over z, x).
Axes of the slice: x: 4, y: 4, z: 4, core: 2. Of those that a mesh axis runs over, the one named last changes fastest.
Arguments:
- queries: bfloat16 [32768, 2048], P(('seq', 'nbr')), may hold values from -16 to 16
- cotangent: bfloat16 [32768, 2048], P(('seq', 'nbr')), may hold values from -6 to 6
- neighbour_tokens: bfloat16 [1024, 128, 896], P(('seq', 'nbr')), may hold values from -6 to 6
- neighbour_ids: int32 [512, 2], P(('seq', 'nbr')), may hold values from 0 to 1023, as said below
- neighbour_dest: int32 [1024], P(('seq', 'nbr')), may hold values from 0 to 1023, as said below
- sequence_ids: int32 [512], P(('seq', 'nbr')), may hold values from 0 to 31, never falling along the last dimension, each value on 1 to 32 neighbouring positions
- enc_in: bfloat16 [896, 1792], replicated, may hold values from -0.1875 to 0.1875
- enc_out: bfloat16 [1792, 896], replicated, may hold values from -0.125 to 0.125
- key_weight: bfloat16 [896, 2048], replicated, may hold values from -0.5 to 0.5
- value_weight: bfloat16 [896, 2048], replicated, may hold values from -0.1875 to 0.1875
Outputs:
- attended: bfloat16 [32768, 2048], P(('seq', 'nbr'))
- grad_encoded: bfloat16 [1024, 128, 896], P(('seq', 'nbr'))
Inputs may be any that keep to these rules, and one draw needn't show every extreme that they name: `neighbour_ids`: every number 0 to 1023 appears exactly once. Neighbour n is held by device n // 8 in the order seq+nbr, a device of the same seq index as the device holding the span. Among the neighbours of one device's spans at most 2 are held by any one device, and in every draw some device has exactly 2 held by one device. neighbour_dest[neighbour_ids[c, k]] = c * 2 + k for every span c and k.
All inputs are finite; a program needn't handle non-finite values.
Results may differ from a plain program's by a relative error of at most 0.015.
The roundings to bfloat16 on the way count: a program that leaves them out, or rounds other values in their place, can miss the bound.
Values may be sent and summed in bfloat16 or wider, within the bound.
No kernel may reach another device: no remote copies, remote signals or barrier semaphores. Data moves between devices by JAX's collectives and lax.ppermute only.
A program may use at most 128 MiB of HBM per device.

v0:
```python
import math

import jax
import jax.numpy as jnp
from jax import lax
from jax.sharding import PartitionSpec as P

HEAD_DIM = 128
CAP = 2


epsilon = 1e-06


def from_behind(block, axis, distance):
    devices = range(lax.axis_size(axis))
    route = [(i - distance, i) for i in devices if i - distance in devices]
    return lax.ppermute(block, axis, route)


def encode(block, enc_in, enc_out):
    inputs = block.astype(jnp.float32)
    scaling = lax.rsqrt(jnp.mean(inputs * inputs, axis=-1, keepdims=True) + epsilon)
    normed = (inputs * scaling).astype(jnp.bfloat16)
    hidden_act = jax.nn.gelu(
        jnp.dot(normed, enc_in, preferred_element_type=jnp.float32), approximate=True
    ).astype(jnp.bfloat16)
    return (inputs + jnp.dot(hidden_act, enc_out, preferred_element_type=jnp.float32)).astype(
        jnp.bfloat16
    )


def attend(query_rows, cot_rows, slot_block, validity, key_weight, value_weight):
    blocks, span_len, features = query_rows.shape
    head_count = features // HEAD_DIM
    slot_count, length, enc_width = slot_block.shape
    flat_slots = slot_block.reshape(slot_count * length, enc_width)
    key_rows = jnp.dot(flat_slots, key_weight, preferred_element_type=jnp.float32).astype(
        jnp.bfloat16
    )
    value_rows = jnp.dot(flat_slots, value_weight, preferred_element_type=jnp.float32).astype(
        jnp.bfloat16
    )
    key_rows = key_rows.reshape(blocks, -1, head_count, HEAD_DIM)
    value_rows = value_rows.reshape(blocks, -1, head_count, HEAD_DIM)
    query_four = query_rows.reshape(blocks, span_len, head_count, HEAD_DIM)
    inv_root = 1.0 / math.sqrt(HEAD_DIM)
    scores = (
        jnp.einsum("cmhd,cphd->chmp", query_four, key_rows, preferred_element_type=jnp.float32)
        * inv_root
    )
    shares = jax.nn.softmax(scores, axis=-1)
    weights = shares.astype(jnp.bfloat16)
    mixture = jnp.einsum("chmp,cphd->cmhd", weights, value_rows, preferred_element_type=jnp.float32)
    attended = (
        (mixture * validity[:, :, None, None])
        .astype(jnp.bfloat16)
        .reshape(blocks, span_len, features)
    )
    masked = (
        cot_rows.reshape(blocks, span_len, head_count, HEAD_DIM)
        * validity.astype(jnp.bfloat16)[:, :, None, None]
    )
    grad_weights = jnp.einsum(
        "cmhd,cphd->chmp", masked, value_rows, preferred_element_type=jnp.float32
    )
    grad_scores = (
        shares * (grad_weights - jnp.sum(shares * grad_weights, axis=-1, keepdims=True))
    ).astype(jnp.bfloat16)
    grad_keys = (
        jnp.einsum("chmp,cmhd->cphd", grad_scores, query_four, preferred_element_type=jnp.float32)
        * inv_root
    ).astype(jnp.bfloat16)
    grad_values = jnp.einsum(
        "chmp,cmhd->cphd", weights, masked, preferred_element_type=jnp.float32
    ).astype(jnp.bfloat16)
    grad_keys = grad_keys.reshape(slot_count * length, features)
    grad_values = grad_values.reshape(slot_count * length, features)
    slot_grads = jnp.dot(grad_keys, key_weight.T, preferred_element_type=jnp.float32) + jnp.dot(
        grad_values, value_weight.T, preferred_element_type=jnp.float32
    )
    return (attended, slot_grads.astype(jnp.bfloat16).reshape(slot_count, length, enc_width))


def shards(
    queries,
    cotangent,
    neighbour_tokens,
    neighbour_ids,
    neighbour_dest,
    sequence_ids,
    enc_in,
    enc_out,
    key_weight,
    value_weight,
):
    span_count = sequence_ids.shape[0]
    token_rows, features = queries.shape
    span_len = token_rows // span_count
    head_rows = span_len - 1
    nb_local, length, enc_width = neighbour_tokens.shape
    peer_count = lax.axis_size("nbr")
    slot_total = peer_count * CAP
    label_send = (sequence_ids[:1] % 128 + 1).astype(jnp.bfloat16)
    next_query, next_cot, next_label = from_behind(
        (queries[:head_rows], cotangent[:head_rows], label_send), ("seq", "nbr"), -1
    )
    own_label = (sequence_ids % 128 + 1).astype(jnp.bfloat16)
    later_label = jnp.concatenate([own_label[1:], next_label], 0)
    offsets = jnp.arange(span_len)
    validity = ((offsets[None, :] == 0) | (own_label[:, None] == later_label[:, None])).astype(
        jnp.float32
    )
    query_ext = jnp.concatenate([queries[head_rows:], next_query], 0).reshape(
        span_count, span_len, features
    )
    cot_ext = jnp.concatenate([cotangent[head_rows:], next_cot], 0).reshape(
        span_count, span_len, features
    )
    encoded = encode(
        neighbour_tokens.reshape(nb_local * length, enc_width), enc_in, enc_out
    ).reshape(nb_local, length, enc_width)
    slot_ids = neighbour_ids.reshape(-1) % (peer_count * nb_local)
    owners = slot_ids // nb_local
    same_owner = (owners[:, None] == owners[None, :]) & (slot_ids[None, :] < slot_ids[:, None])
    recv_slot = owners * CAP + jnp.sum(same_owner.astype(jnp.int32), axis=1)
    dest_peer = neighbour_dest // nb_local % peer_count
    earlier = jnp.arange(nb_local)
    same_dest = (dest_peer[:, None] == dest_peer[None, :]) & (earlier[None, :] < earlier[:, None])
    send_slot = dest_peer * CAP + jnp.sum(same_dest.astype(jnp.int32), axis=1)
    slot_index = jnp.arange(slot_total)
    send_table = (slot_index[:, None] == send_slot[None, :]).astype(jnp.bfloat16)
    outgoing = jnp.dot(
        send_table, encoded.reshape(nb_local, -1), preferred_element_type=jnp.float32
    )
    outgoing = outgoing.astype(jnp.bfloat16).reshape(slot_total, length, enc_width)
    incoming = lax.all_to_all(outgoing, "nbr", split_axis=0, concat_axis=0, tiled=True)
    slot_block = jnp.take(incoming, recv_slot, axis=0)
    attended_ext, slot_grads = attend(
        query_ext, cot_ext, slot_block, validity, key_weight, value_weight
    )
    recv_table = (slot_index[:, None] == recv_slot[None, :]).astype(jnp.bfloat16)
    outgoing_grads = jnp.dot(
        recv_table, slot_grads.reshape(nb_local, -1), preferred_element_type=jnp.float32
    )
    outgoing_grads = outgoing_grads.astype(jnp.bfloat16).reshape(slot_total, length, enc_width)
    returned = lax.all_to_all(outgoing_grads, "nbr", split_axis=0, concat_axis=0, tiled=True)
    grad_encoded = jnp.take(returned, send_slot, axis=0)
    extended = attended_ext.reshape(token_rows, features)
    carried = from_behind(extended[token_rows - head_rows :], ("seq", "nbr"), 1)
    attended = jnp.concatenate([carried, extended[: token_rows - head_rows]], 0)
    return (attended, grad_encoded)


def solution(mesh):
    in_specs = (
        P(("seq", "nbr"), None),
        P(("seq", "nbr"), None),
        P(("seq", "nbr"), None, None),
        P(("seq", "nbr"), None),
        P(("seq", "nbr")),
        P(("seq", "nbr")),
        P(),
        P(),
        P(),
        P(),
    )
    out_specs = (P(("seq", "nbr"), None), P(("seq", "nbr"), None, None))
    return jax.shard_map(shards, mesh=mesh, in_specs=in_specs, out_specs=out_specs, check_vma=False)
```

profile of v0, /device:TPU:14, one launch (start us, length us, event | category | flops | bytes accessed | tf_op | source)
XLA Modules:
  0.0 386.5 jit_solution(11268373625529754706)
XLA Ops:
  4.3 3.1 fusion.24
  7.4 11.4 %fusion.25 = bf16[1024,896]{1,0:T(8,128)(2,1)} fusion(bf16[8,128,896]{2,1,0:T(8,128)(2,1)} %param.14, bf16[1792,896]{1,0:T(8,128)(2,1)S(1)} %copy-done, bf16[1024,896]{1,0:T(8,128)(2,1)} %fusion.24, bf16[896,1792]{1,0:T(8,128)(2,1)} %param.18), kind=kOutput, calls=%fused_computation.41 | convolution fusion | flops 6595936256 | bytes 11927552 | tf_op jit(solution)/shard_map/dot_general | solution.py:28
  23.2 4.4 %copy.38 = bf16[4,8,128,896]{3,2,1,0:T(8,128)(2,1)} copy(bf16[4,8,128,896]{3,1,2,0:T(8,128)(2,1)S(1)} %bitcast.68) | data formatting | bytes 14680064
  27.6 8.4 %all-to-all-start = ((bf16[32,128,896]{2,1,0:T(8,128)(2,1)}), bf16[32,128,896]{2,1,0:T(8,128)(2,1)}, u32[]{:S(2)}, u32[]{:S(2)}) async-start(bf16[32,128,896]{2,1,0:T(8,128)(2,1)} %bitcast.65), calls=%async_computation | async-start | bytes 14680064 | tf_op jit(solution)/shard_map/all_to_all | solution.py:137
  36.1 98.5 %collective-permute-start.1 = (bf16[1]{0:T(256)(128)(2,1)}, bf16[1]{0:T(256)(128)(2,1)}, u32[]{:S(2)}, u32[]{:S(2)}) collective-permute-start(bf16[1]{0:T(256)(128)(2,1)} %convert_element_type.101), channel_id=1, source_target_pairs={{1,0},{2,1},{3,2},{4,3},{5,4},{6,5},{7,6},{8,7},{9,8},{10,9},{11,1... | collective-permute-start | bytes 14 | tf_op jit(solution)/shard_map/ppermute | solution.py:18
  136.6 10.3 %collective-permute-start = (bf16[63,2048]{1,0:T(8,128)(2,1)S(1)}, bf16[63,2048]{1,0:T(8,128)(2,1)}, u32[]{:S(2)}, u32[]{:S(2)}) collective-permute-start(bf16[63,2048]{1,0:T(8,128)(2,1)S(1)} %slice.25), channel_id=1, source_target_pairs={{1,0},{2,1},{3,2},{4,3},{5,4},{6,5},{7,6},{8,7},{9,8},{10,9},{11,1... | collective-permute-start | bytes 774152 | tf_op jit(solution)/shard_map/ppermute | solution.py:18
  149.6 4.3 %collective-permute-done = bf16[63,2048]{1,0:T(8,128)(2,1)} collective-permute-done((bf16[63,2048]{1,0:T(8,128)(2,1)S(1)}, bf16[63,2048]{1,0:T(8,128)(2,1)}, u32[]{:S(2)}, u32[]{:S(2)}) %collective-permute-start) | collective-permute-done | bytes 258080 | tf_op jit(solution)/shard_map/ppermute | solution.py:18
  157.5 3.9 %gather_fusion = bf16[8,128,896]{2,1,0:T(8,128)(2,1)S(1)} fusion(bf16[32,128,896]{2,1,0:T(8,128)(2,1)} %all-to-all-done, s32[1024]{0:T(1024)S(1)} %pad_clamp_fusion.1), kind=kCustom, calls=%fused_computation.clone | custom fusion | bytes 3670048 | tf_op jit(solution)/shard_map/jit(_take)/gather | solution.py:138
  161.7 6.8 %convert_bitcast_fusion.1 = bf16[128,8,16,128]{3,1,2,0:T(8,128)(2,1)S(1)} fusion(bf16[1024,896]{1,0:T(8,128)(2,1)S(1)} %bitcast.79, bf16[896,2048]{1,0:T(8,128)(2,1)} %param.20), kind=kOutput, calls=%fused_computation.28 | convolution fusion | flops 3760193536 | bytes 9699328 | tf_op jit(solution)/shard_map/dot_general | solution.py:38
  170.6 4.7 %convert_bitcast_fusion.2 = bf16[128,8,16,128]{3,1,2,0:T(8,128)(2,1)S(1)} fusion(bf16[1024,896]{1,0:T(8,128)(2,1)S(1)} %bitcast.80, bf16[896,2048]{1,0:T(8,128)(2,1)S(1)} %copy-done.11), kind=kOutput, calls=%fused_computation.29 | convolution fusion | flops 3760193536 | bytes 9699328 | tf_op jit(solution)/shard_map/dot_general | solution.py:41
  175.3 3.4 copy.40
  183.5 12.7 %convert_bitcast_fusion = bf16[4,256,16,128]{1,3,2,0:T(8,128)(2,1)} fusion(bf16[4,64,16,128]{3,2,1,0:T(8,128)(2,1)S(1)} %bitcast.81, bf16[4,64]{1,0:T(4,128)(2,1)S(1)} %get-tuple-element.9, f32[4,16,64]{2,1,0:T(8,128)S(1)} %get-tuple-element.11, f32[4,16,64,256]{3,2,1,0:T(8,128)} %copy-done.2), kind=kOutput, calls=%fused_computation.24 | convolution fusion | flops 276304128 | bytes 9454080 | tf_op jit(solution)/shard_map/chmp,cmhd->cphd/dot_general | solution.py:74
  196.2 8.0 %copy.36 = bf16[4,256,16,128]{3,2,1,0:T(8,128)(2,1)} copy(bf16[4,256,16,128]{1,3,2,0:T(8,128)(2,1)} %convert_bitcast_fusion) | data formatting | bytes 8388608 | tf_op jit(solution)/shard_map/convert_element_type | solution.py:76
  204.3 9.8 %fusion.10 = f32[1024,896]{1,0:T(8,128)} fusion(bf16[896,2048]{1,0:T(8,128)(2,1)} %param.21, bf16[128,8,16,128]{3,2,1,0:T(8,128)(2,1)} %bitcast.77), kind=kOutput, calls=%fused_computation.16 | convolution fusion | flops 3758096384 | bytes 11534336 | tf_op jit(solution)/shard_map/dot_general | solution.py:79
  214.1 3.7 multiply_reduce_fusion
  217.9 14.5 %fusion.9 = bf16[4,256,16,128]{1,3,2,0:T(8,128)(2,1)} fusion(f32[4,16,64,256]{3,2,1,0:T(8,128)} %get-tuple-element.14, f32[4,16,64]{2,1,0:T(8,128)S(1)} %get-tuple-element.13, bf16[4,64,16,128]{3,2,1,0:T(8,128)(2,1)S(1)} %bitcast.73, f32[4,16,64]{2,1,0:T(8,128)S(1)} %get-tuple-element.11, f32[4,16,64,256]{3,2,1,0:T(8,128)} %copy-done.2), kind=kOutput, calls=%fused_computation.15 | convolution fusion | flops 279974144 | bytes 13664256 | tf_op jit(solution)/shard_map/chmp,cmhd->cphd/dot_general | solution.py:71
  232.4 8.1 %copy.35 = bf16[4,256,16,128]{3,2,1,0:T(8,128)(2,1)} copy(bf16[4,256,16,128]{1,3,2,0:T(8,128)(2,1)} %fusion.9) | data formatting | bytes 8388608 | tf_op jit(solution)/shard_map/convert_element_type | solution.py:73
  240.5 10.1 %add_convert_fusion = bf16[1024,896]{1,0:T(8,128)(2,1)} fusion(f32[1024,896]{1,0:T(8,128)} %fusion.10, bf16[896,2048]{1,0:T(8,128)(2,1)} %param.20, bf16[128,8,16,128]{3,2,1,0:T(8,128)(2,1)} %bitcast.76), kind=kOutput, calls=%fused_computation.42 | convolution fusion | flops 3759931392 | bytes 13369344 | tf_op jit(solution)/shard_map/dot_general | solution.py:79
  254.9 4.4 %copy.45 = bf16[4,8,128,896]{3,2,1,0:T(8,128)(2,1)} copy(bf16[4,8,128,896]{3,1,2,0:T(8,128)(2,1)S(1)} %bitcast.67) | data formatting | bytes 14680064
  259.3 8.4 %all-to-all-start.1 = ((bf16[32,128,896]{2,1,0:T(8,128)(2,1)}), bf16[32,128,896]{2,1,0:T(8,128)(2,1)}, u32[]{:S(2)}, u32[]{:S(2)}) async-start(bf16[32,128,896]{2,1,0:T(8,128)(2,1)} %bitcast.66), calls=%async_computation.1 | async-start | bytes 14680064 | tf_op jit(solution)/shard_map/all_to_all | solution.py:147
  267.8 12.1 %fusion.38 = bf16[4,64,16,128]{3,1,2,0:T(8,128)(2,1)S(1)} fusion(bf16[4,256,16,128]{3,2,1,0:T(8,128)(2,1)} %bitcast.74, f32[4,64]{1,0:T(4,128)S(1)} %get-tuple-element.10, f32[4,16,64]{2,1,0:T(8,128)S(1)} %get-tuple-element.11, f32[4,16,64,256]{3,2,1,0:T(8,128)} %copy-done.2), kind=kOutput, calls=%fused_computation.50 | convolution fusion | flops 274731264 | bytes 9454592 | tf_op jit(solution)/shard_map/chmp,cphd->cmhd/dot_general | solution.py:54
  280.9 3.4 collective-permute-start.2
  284.4 92.3 %collective-permute-done.2 = bf16[63,2048]{1,0:T(8,128)(2,1)S(1)} collective-permute-done((bf16[63,2048]{1,0:T(8,128)(2,1)S(1)}, bf16[63,2048]{1,0:T(8,128)(2,1)S(1)}, u32[]{:S(2)}, u32[]{:S(2)}) %collective-permute-start.2) | collective-permute-done | bytes 258080 | tf_op jit(solution)/shard_map/ppermute | solution.py:18
  377.9 5.2 %gather_fusion.1 = bf16[8,128,896]{2,1,0:T(8,128)(2,1)} fusion(bf16[32,128,896]{2,1,0:T(8,128)(2,1)} %all-to-all-done.1, s32[1024]{0:T(1024)S(1)} %pad_clamp_fusion), kind=kCustom, calls=%fused_computation.1.clone | custom fusion | bytes 3670048 | tf_op jit(solution)/shard_map/jit(_take)/gather | solution.py:148
  (70 shorter events, 32.9 us)
Async XLA Ops:
  0.6 6.7 %copy-start = (bf16[1792,896]{1,0:T(8,128)(2,1)S(1)}, bf16[1792,896]{1,0:T(8,128)(2,1)}, u32[]{:S(2)}) copy-start(bf16[1792,896]{1,0:T(8,128)(2,1)} %param.19) | copy-start | bytes 9633796
  27.6 8.4 %copy-start.9 = (s32[4]{0:T(128)S(1)}, s32[4]{0:T(128)}, u32[]{:S(2)}) copy-start(s32[4]{0:T(128)} %param.17) | copy-start | bytes 52
  27.6 107.1 %copy-start.7 = (bf16[256,2048]{1,0:T(8,128)(2,1)S(1)}, bf16[256,2048]{1,0:T(8,128)(2,1)}, u32[]{:S(2)}) copy-start(bf16[256,2048]{1,0:T(8,128)(2,1)} %param.13) | copy-start | bytes 3145732
  27.6 109.0 %copy-start.6 = (bf16[256,2048]{1,0:T(8,128)(2,1)S(1)}, bf16[256,2048]{1,0:T(8,128)(2,1)}, u32[]{:S(2)}) copy-start(bf16[256,2048]{1,0:T(8,128)(2,1)} %param.12) | copy-start | bytes 3145732
  27.6 129.9 %all-to-all-start = ((bf16[32,128,896]{2,1,0:T(8,128)(2,1)}), bf16[32,128,896]{2,1,0:T(8,128)(2,1)}, u32[]{:S(2)}, u32[]{:S(2)}) async-start(bf16[32,128,896]{2,1,0:T(8,128)(2,1)} %bitcast.65), calls=%async_computation | async-start | bytes 14680064 | tf_op jit(solution)/shard_map/all_to_all | solution.py:137
  36.0 112.4 %copy-start.10 = (s32[4,2]{0,1:T(2,128)S(1)}, s32[4,2]{0,1:T(2,128)}, u32[]{:S(2)}) copy-start(s32[4,2]{0,1:T(2,128)} %param.15) | copy-start | bytes 100
  36.1 112.7 %collective-permute-start.1 = (bf16[1]{0:T(256)(128)(2,1)}, bf16[1]{0:T(256)(128)(2,1)}, u32[]{:S(2)}, u32[]{:S(2)}) collective-permute-start(bf16[1]{0:T(256)(128)(2,1)} %convert_element_type.101), channel_id=1, source_target_pairs={{1,0},{2,1},{3,2},{4,3},{5,4},{6,5},{7,6},{8,7},{9,8},{10,9},{11,1... | collective-permute-start | bytes 14 | tf_op jit(solution)/shard_map/ppermute | solution.py:18
  134.7 20.5 %collective-permute-start.3 = (bf16[63,2048]{1,0:T(8,128)(2,1)S(1)}, bf16[63,2048]{1,0:T(8,128)(2,1)}, u32[]{:S(2)}, u32[]{:S(2)}) collective-permute-start(bf16[63,2048]{1,0:T(8,128)(2,1)S(1)} %slice.31), channel_id=1, source_target_pairs={{1,0},{2,1},{3,2},{4,3},{5,4},{6,5},{7,6},{8,7},{9,8},{10,9},{11,1... | collective-permute-start | bytes 774152 | tf_op jit(solution)/shard_map/ppermute | solution.py:18
  136.6 17.2 %collective-permute-start = (bf16[63,2048]{1,0:T(8,128)(2,1)S(1)}, bf16[63,2048]{1,0:T(8,128)(2,1)}, u32[]{:S(2)}, u32[]{:S(2)}) collective-permute-start(bf16[63,2048]{1,0:T(8,128)(2,1)S(1)} %slice.25), channel_id=1, source_target_pairs={{1,0},{2,1},{3,2},{4,3},{5,4},{6,5},{7,6},{8,7},{9,8},{10,9},{11,1... | collective-permute-start | bytes 774152 | tf_op jit(solution)/shard_map/ppermute | solution.py:18
  148.5 6.7 %copy-start.5 = (bf16[193,2048]{1,0:T(8,128)(2,1)S(1)}, bf16[193,2048]{1,0:T(8,128)(2,1)}, u32[]{:S(2)}) copy-start(bf16[193,2048]{1,0:T(8,128)(2,1)} %slice.30) | copy-start | bytes 2371588
  168.5 2.0 copy-start.11
  180.2 3.3 copy-start.2
  180.2 3.3 copy-start.8
  204.3 9.9 %copy-start.3 = (bf16[128,8,16,128]{3,2,1,0:T(8,128)(2,1)S(1)}, bf16[128,8,16,128]{3,2,1,0:T(8,128)(2,1)}, u32[]{:S(2)}) copy-start(bf16[128,8,16,128]{3,2,1,0:T(8,128)(2,1)} %copy.40) | copy-start | bytes 12582916
  204.3 9.9 %copy-start.4 = (f32[4,16,64,256]{3,2,1,0:T(8,128)S(1)}, f32[4,16,64,256]{3,2,1,0:T(8,128)}, u32[]{:S(2)}) copy-start(f32[4,16,64,256]{3,2,1,0:T(8,128)} %get-tuple-element.12) | copy-start | bytes 12582916
  259.3 118.5 %all-to-all-start.1 = ((bf16[32,128,896]{2,1,0:T(8,128)(2,1)}), bf16[32,128,896]{2,1,0:T(8,128)(2,1)}, u32[]{:S(2)}, u32[]{:S(2)}) async-start(bf16[32,128,896]{2,1,0:T(8,128)(2,1)} %bitcast.66), calls=%async_computation.1 | async-start | bytes 14680064 | tf_op jit(solution)/shard_map/all_to_all | solution.py:147
  280.9 95.8 %collective-permute-start.2 = (bf16[63,2048]{1,0:T(8,128)(2,1)S(1)}, bf16[63,2048]{1,0:T(8,128)(2,1)S(1)}, u32[]{:S(2)}, u32[]{:S(2)}) collective-permute-start(bf16[63,2048]{1,0:T(8,128)(2,1)S(1)} %slice.36), channel_id=1, source_target_pairs={{0,1},{1,2},{2,3},{3,4},{4,5},{5,6},{6,7},{7,8},{8,9},{9,10},{10,1... | collective-permute-start | bytes 774152 | tf_op jit(solution)/shard_map/ppermute | solution.py:18
  376.6 9.4 %copy-start.1 = (bf16[1792,896]{1,0:T(8,128)(2,1)S(1)}, bf16[1792,896]{1,0:T(8,128)(2,1)}, u32[]{:S(2)}) copy-start(bf16[1792,896]{1,0:T(8,128)(2,1)} %param.19) | copy-start | bytes 9633796
where the time goes:
time: 394 us; the launch traced here: 387 us
  starting transfers between devices  131 us (33%)
  waiting for transfers between devices  96.5 us (24%)
  matrix products  91.6 us (23%)
  local copies, waits for them, and re-layouts  48.7 us (12%)
  other arithmetic  17.2 us (4%)
    ppermute x4, starting transfers between devices, from_behind(): return lax.ppermute(block, axis, route)  114 us
    ppermute x4, waiting for transfers between devices, from_behind(): return lax.ppermute(block, axis, route)  96.5 us
    unnamed x32, local copies, waits for them, and re-layouts  16.5 us
    dot_general x1, matrix products, attend(): jnp.einsum('chmp,cmhd->cphd', grad_scores, query_four, preferred_element_...  14.5 us
    dot_general x1, matrix products, attend(): jnp.einsum('chmp,cmhd->cphd', weights, masked, preferred_element_type=jnp...  12.7 us
    dot_general x1, matrix products, attend(): jnp.einsum('chmp,cphd->cmhd', weights, value_rows, preferred_element_type...  12.1 us
    dot_general x1, matrix products, encode(): jnp.dot(hidden_act, enc_out, preferred_element_type=jnp.float32)  11.4 us
    dot_general x1, matrix products, attend(): jnp.dot(grad_keys, key_weight.T, preferred_element_type=jnp.float32)  10.1 us
  transfers between devices with their start and end apart: 6, of which 2 were waited for; matrix products, arithmetic and copies ran while one was open for 5% of the time, Pallas kernels for 0%

commit v1 on v0

v1 whole, which is shorter than its diff:
```python
import math

import jax
import jax.numpy as jnp
from jax import lax
from jax.experimental import pallas as pl
from jax.experimental.pallas import tpu as pltpu
from jax.sharding import PartitionSpec as P

HEAD = 128
EPS = 1e-06
PIECE = 8
NT = (((1,), (1,)), ((), ()))
TN = (((0,), (0,)), ((), ()))
F32 = jnp.float32
BF16 = jnp.bfloat16
VMEM_LIMIT = 56 * 1024 * 1024


def params(n=1):
    return pltpu.CompilerParams(
        dimension_semantics=("arbitrary",) * n, vmem_limit_bytes=VMEM_LIMIT
    )


def from_behind(block, axis, distance):
    devices = range(lax.axis_size(axis))
    route = [(i - distance, i) for i in devices if i - distance in devices]
    return lax.ppermute(block, axis, route)


def spread(block):
    return lax.all_to_all(block, "nbr", split_axis=0, concat_axis=0, tiled=True)


def encode_kernel(tok_ref, ids_ref, win_ref, wout_ref, out_ref, normed, acc):
    step = pl.program_id(0)
    count, length, width = tok_ref.shape
    pieces = length // PIECE

    @pl.when(step == 0)
    def _():
        for i in range(count):
            x = tok_ref[i].astype(F32)
            scale = lax.rsqrt(jnp.mean(x * x, axis=-1, keepdims=True) + EPS)
            normed[pl.ds(i * length, length), :] = (x * scale).astype(BF16)
            acc[pl.ds(i * length, length), :] = x

    rows = 256
    for b in range(count * length // rows):
        at = pl.ds(b * rows, rows)
        hidden = jnp.dot(normed[at, :], win_ref[...], preferred_element_type=F32)
        hidden = jax.nn.gelu(hidden, approximate=True).astype(BF16)
        acc[at, :] += jnp.dot(hidden, wout_ref[...], preferred_element_type=F32)

    @pl.when(step == pl.num_programs(0) - 1)
    def _():
        for i in range(count):
            y = acc[pl.ds(i * length, length), :].astype(BF16)
            out_ref[:, i] = y.reshape(pieces, PIECE, width)
        for p in range(pieces):
            out_ref[p, count] = ids_ref[...]


def encode(tokens, ids, enc_in, enc_out):
    count, length, width = tokens.shape
    hidden = enc_in.shape[1]
    block = 256
    pieces = length // PIECE
    return pl.pallas_call(
        encode_kernel,
        grid=(hidden // block,),
        in_specs=[
            pl.BlockSpec((count, length, width), lambda f: (0, 0, 0)),
            pl.BlockSpec((PIECE, width), lambda f: (0, 0)),
            pl.BlockSpec((width, block), lambda f: (0, f)),
            pl.BlockSpec((block, width), lambda f: (f, 0)),
        ],
        out_specs=pl.BlockSpec((pieces, count + 1, PIECE, width), lambda f: (0, 0, 0, 0)),
        out_shape=jax.ShapeDtypeStruct((pieces, count + 1, PIECE, width), BF16),
        scratch_shapes=[
            pltpu.VMEM((count * length, width), BF16),
            pltpu.VMEM((count * length, width), F32),
        ],
        compiler_params=params(),
        name="encode",
    )(tokens, ids, enc_in, enc_out)


def reorder_kernel(inverse, table_ref, src_ref, dst_ref, sem):
    peers, count = dst_ref.shape[:2]

    def body(k, carry):
        at = table_ref[k]
        there = (at // count, at % count)
        here = (k // count, k % count)
        a, b = (here, there) if inverse else (there, here)
        pltpu.make_async_copy(src_ref.at[a[0], a[1]], dst_ref.at[b[0], b[1]], sem).start()
        return carry

    lax.fori_loop(0, peers * count, body, 0, unroll=8)
    pltpu.make_async_copy(src_ref.at[:, :count], dst_ref, sem).wait()


def reorder(table, block, count, inverse):
    return pl.pallas_call(
        lambda *refs: reorder_kernel(inverse, *refs),
        grid_spec=pltpu.PrefetchScalarGridSpec(
            num_scalar_prefetch=1,
            in_specs=[pl.BlockSpec(memory_space=pltpu.VMEM)],
            out_specs=pl.BlockSpec(memory_space=pl.ANY),
            scratch_shapes=[pltpu.SemaphoreType.DMA],
        ),
        out_shape=jax.ShapeDtypeStruct(block.shape[:1] + (count,) + block.shape[2:], block.dtype),
        compiler_params=pltpu.CompilerParams(vmem_limit_bytes=VMEM_LIMIT),
        name="reorder_back" if inverse else "reorder",
    )(table, block)


def regroup_kernel(src_ref, dst_ref, sem):
    copies = [
        pltpu.make_async_copy(src_ref.at[:, i], dst_ref.at[i], sem.at[i])
        for i in range(dst_ref.shape[0])
    ]
    for copy in copies:
        copy.start()
    for copy in copies:
        copy.wait()


def regroup(block):
    pieces, count, rows, width = block.shape
    out = pl.pallas_call(
        regroup_kernel,
        in_specs=[pl.BlockSpec(memory_space=pltpu.VMEM)],
        out_specs=pl.BlockSpec(memory_space=pl.ANY),
        out_shape=jax.ShapeDtypeStruct((count, pieces, rows, width), block.dtype),
        scratch_shapes=[pltpu.SemaphoreType.DMA((count,))],
        name="regroup",
    )(block)
    return out.reshape(count, pieces * rows, width)


def span_rows(own, later, span):
    last = lax.broadcasted_iota(jnp.int32, (span, own.shape[1]), 0) == span - 1
    blocks = own.shape[0] // span
    out = []
    for c in range(blocks):
        here = own[c * span : (c + 1) * span]
        after = own[(c + 1) * span : (c + 2) * span] if c + 1 < blocks else later
        out.append(jnp.where(last, here, after))
    return out


def row_valid(valid_ref, c, span, width):
    last = lax.broadcasted_iota(jnp.int32, (span, width), 0) == span - 1
    return jnp.where(last, 1.0, valid_ref[c].astype(F32))


def project_kernel(valid_ref, q_ref, nq_ref, g_ref, ng_ref, wk_ref, wv_ref, qw_ref, mw_ref):
    spans, heads, span, width = qw_ref.shape
    inv_root = 1.0 / math.sqrt(HEAD)
    q = span_rows(q_ref[...].astype(F32), nq_ref[...].astype(F32), span)
    g = span_rows(g_ref[...].astype(F32), ng_ref[...].astype(F32), span)
    g = [g[c] * row_valid(valid_ref, c, span, g[c].shape[1]) for c in range(spans)]
    q = jnp.concatenate(q, 0).astype(BF16)
    g = jnp.concatenate(g, 0).astype(BF16)
    for h in range(heads):
        at = slice(h * HEAD, (h + 1) * HEAD)
        qw = lax.dot_general(q[:, at], wk_ref[:, at], NT, preferred_element_type=F32)
        qw_ref[:, h] = (qw * inv_root).astype(BF16).reshape(spans, span, width)
        mw = lax.dot_general(g[:, at], wv_ref[:, at], NT, preferred_element_type=F32)
        mw_ref[:, h] = mw.astype(BF16).reshape(spans, span, width)


def project(valid, queries, next_query, cotangent, next_cot, key_weight, value_weight, span):
    rows, features = queries.shape
    width = key_weight.shape[0]
    spans = rows // span
    heads = 2
    block = heads * HEAD
    tall = pl.BlockSpec((rows, block), lambda f, v: (0, f))
    short = pl.BlockSpec((span, block), lambda f, v: (0, f))
    wide = pl.BlockSpec((width, block), lambda f, v: (0, f))
    out = pl.BlockSpec((spans, heads, span, width), lambda f, v: (0, f, 0, 0))
    shape = jax.ShapeDtypeStruct((spans, features // HEAD, span, width), BF16)
    return pl.pallas_call(
        project_kernel,
        grid_spec=pltpu.PrefetchScalarGridSpec(
            num_scalar_prefetch=1,
            grid=(features // block,),
            in_specs=[tall, short, tall, short, wide, wide],
            out_specs=[out, out],
        ),
        out_shape=[shape, shape],
        compiler_params=params(),
        name="project",
    )(valid, queries, next_query, cotangent, next_cot, key_weight, value_weight)


def attend_kernel(x_ref, qw_ref, mw_ref, grad_ref, weight_ref):
    pieces, _, rows, width = x_ref.shape
    x = x_ref[:, 0].reshape(pieces * rows, width)
    columns = qw_ref.shape[1]
    block = 256
    total = None
    for b in range(columns // block):
        at = slice(b * block, (b + 1) * block)
        qw = qw_ref[0, at, :]
        mw = mw_ref[0, at, :]
        scores = lax.dot_general(x, qw, NT, preferred_element_type=F32)
        grad_weights = lax.dot_general(x, mw, NT, preferred_element_type=F32)
        shares = jnp.exp(scores - jnp.max(scores, axis=0, keepdims=True))
        shares = shares * (1.0 / jnp.sum(shares, axis=0, keepdims=True))
        weights = shares.astype(BF16)
        inner = jnp.sum(shares * grad_weights, axis=0, keepdims=True)
        grad_scores = (shares * (grad_weights - inner)).astype(BF16)
        weight_ref[0, :, at] = weights
        part = jnp.dot(grad_scores, qw, preferred_element_type=F32) + jnp.dot(
            weights, mw, preferred_element_type=F32
        )
        total = part if total is None else total + part
    grad_ref[:, 0] = total.astype(BF16).reshape(pieces, rows, width)


def attend(slots, qw, mw):
    pieces, spans, rows, width = slots.shape
    columns = qw.shape[1]
    piece = pl.BlockSpec((pieces, 1, rows, width), lambda c: (0, c, 0, 0))
    projected = pl.BlockSpec((1, columns, width), lambda c: (c, 0, 0))
    return pl.pallas_call(
        attend_kernel,
        grid=(spans,),
        in_specs=[piece, projected, projected],
        out_specs=[piece, pl.BlockSpec((1, pieces * rows, columns), lambda c: (c, 0, 0))],
        out_shape=[
            jax.ShapeDtypeStruct(slots.shape, BF16),
            jax.ShapeDtypeStruct((spans, pieces * rows, columns), BF16),
        ],
        compiler_params=params(),
        name="attend",
    )(slots, qw, mw)


def mix_kernel(valid_ref, x_ref, weight_ref, wv_ref, out_ref, tail_ref, before):
    c = pl.program_id(0)
    pieces, _, rows, width = x_ref.shape
    span = out_ref.shape[0]
    x = x_ref[:, 0].reshape(pieces * rows, width)
    pair = 2 * HEAD
    scale = row_valid(valid_ref, c, span, HEAD)
    last = lax.broadcasted_iota(jnp.int32, (span, HEAD), 0) == span - 1
    for b in range(wv_ref.shape[1] // pair):
        values = jnp.dot(x, wv_ref[:, b * pair : (b + 1) * pair], preferred_element_type=F32)
        weights = weight_ref[0, :, b * 2 * span : (b + 1) * 2 * span]
        mixed = lax.dot_general(weights, values.astype(BF16), TN, preferred_element_type=F32)
        for h in range(2):
            at = slice(b * pair + h * HEAD, b * pair + (h + 1) * HEAD)
            now = mixed[h * span : (h + 1) * span, h * HEAD : (h + 1) * HEAD] * scale
            out_ref[:, at] = jnp.where(last, now, before[:, at]).astype(BF16)
            before[:, at] = now

    @pl.when(c == pl.num_programs(0) - 1)
    def _():
        tail_ref[...] = before[...].astype(BF16)


def mix(valid, slots, weights, value_weight, span):
    pieces, spans, rows, width = slots.shape
    features = value_weight.shape[1]
    return pl.pallas_call(
        mix_kernel,
        grid_spec=pltpu.PrefetchScalarGridSpec(
            num_scalar_prefetch=1,
            grid=(spans,),
            in_specs=[
                pl.BlockSpec((pieces, 1, rows, width), lambda c, v: (0, c, 0, 0)),
                pl.BlockSpec((1,) + weights.shape[1:], lambda c, v: (c, 0, 0)),
                pl.BlockSpec((width, features), lambda c, v: (0, 0)),
            ],
            out_specs=[
                pl.BlockSpec((span, features), lambda c, v: (c, 0)),
                pl.BlockSpec((span, features), lambda c, v: (0, 0)),
            ],
            scratch_shapes=[pltpu.VMEM((span, features), F32)],
        ),
        out_shape=[
            jax.ShapeDtypeStruct((spans * span, features), BF16),
            jax.ShapeDtypeStruct((span, features), BF16),
        ],
        compiler_params=params(),
        name="mix",
    )(valid, slots, weights, value_weight)


def join_kernel(whole_ref, carried_ref, out_ref):
    span, features = out_ref.shape
    last = lax.broadcasted_iota(jnp.int32, (span, features), 0) == span - 1
    out_ref[...] = jnp.where(
        last, whole_ref[...].astype(F32), carried_ref[...].astype(F32)
    ).astype(BF16)


def join(whole, carried):
    first = pl.BlockSpec(carried.shape, lambda i: (0, 0))
    return pl.pallas_call(
        join_kernel,
        grid=(1,),
        in_specs=[first, first],
        out_specs=first,
        out_shape=jax.ShapeDtypeStruct(whole.shape, whole.dtype),
        input_output_aliases={0: 0},
        compiler_params=params(),
        name="join",
    )(whole, carried)


def shards(
    queries,
    cotangent,
    neighbour_tokens,
    neighbour_ids,
    neighbour_dest,
    sequence_ids,
    enc_in,
    enc_out,
    key_weight,
    value_weight,
):
    spans = sequence_ids.shape[0]
    rows, features = queries.shape
    span = rows // spans
    count, length, width = neighbour_tokens.shape
    peers = lax.axis_size("nbr")
    everyone = ("seq", "nbr")

    own_ids = (neighbour_ids.reshape(1, count) % (peers * count)).astype(BF16)
    own_ids = jnp.pad(own_ids, ((0, PIECE - 1), (0, width - count)))
    next_label = from_behind(sequence_ids[:1] + 1, everyone, -1)
    next_query = from_behind(queries[:span], everyone, -1)
    next_cot = from_behind(cotangent[:span], everyone, -1)
    labels = sequence_ids + 1
    valid = (labels == jnp.concatenate([labels[1:], next_label], 0)).astype(jnp.int32)

    pieces = encode(neighbour_tokens, own_ids, enc_in, enc_out)
    pieces, next_query, next_cot, valid = lax.optimization_barrier(
        (pieces, next_query, next_cot, valid)
    )
    held = spread(pieces)
    table = held[:, count, 0, :count].astype(jnp.int32).reshape(-1)
    qw, mw = project(
        valid, queries, next_query, cotangent, next_cot, key_weight, value_weight, span
    )
    held, table, qw, mw = lax.optimization_barrier((held, table, qw, mw))
    slots = spread(reorder(table, held, count, False))
    pair = (peers, spans, count // spans * PIECE, width)
    columns = features // HEAD * span
    grads, weights = attend(
        slots.reshape(pair), qw.reshape(spans, columns, width), mw.reshape(spans, columns, width)
    )
    held_grads = spread(grads.reshape(slots.shape))
    whole, tail = mix(valid, slots.reshape(pair), weights, value_weight, span)
    carried = from_behind(tail, everyone, 1)
    attended = join(whole, carried)
    returned = spread(reorder(table, held_grads, count, True))
    return attended, regroup(returned)


def solution(mesh):
    rows = P(("seq", "nbr"), None)
    blocks = P(("seq", "nbr"), None, None)
    flat = P(("seq", "nbr"))
    in_specs = (rows, rows, blocks, rows, flat, flat, P(), P(), P(), P())
    return jax.shard_map(
        shards, mesh=mesh, in_specs=in_specs, out_specs=(rows, blocks), check_vma=False
    )
```

time: 394 us -> 202 us (0.51)
  the two profiles are of different devices: /device:TPU:14 before, /device:TPU:1 now
where the time goes in v1:
time: 202 us; the launch traced here: 201 us
  Pallas kernels  77.4 us (38%)
  blocking collectives  56.3 us (28%)
  waiting for transfers between devices  31.1 us (15%)
  starting transfers between devices  26.3 us (13%)
  local copies, waits for them, and re-layouts  6.71 us (3%)
    all_to_all x2, blocking collectives, spread(): return lax.all_to_all(block, 'nbr', split_axis=0, concat_axis=0, tiled=True)  56.3 us
    ppermute x4, starting transfers between devices, from_behind(): return lax.ppermute(block, axis, route)  18.8 us
    pallas_call x1, Pallas kernels, mix(): pl.pallas_call(mix_kernel, grid_spec=pltpu.PrefetchScalarGridSpec(num_sca...  18 us
    all_to_all x2, waiting for transfers between devices, spread(): return lax.all_to_all(block, 'nbr', split_axis=0, concat_axis=0, tiled=True)  17.4 us
    pallas_call x1, Pallas kernels, attend(): pl.pallas_call(attend_kernel, grid=(spans,), in_specs=[piece, projected,...  16.7 us
    pallas_call x1, Pallas kernels, encode(): pl.pallas_call(encode_kernel, grid=(hidden // block,), in_specs=[pl.Block...  15.3 us
    pallas_call x1, Pallas kernels, project(): pl.pallas_call(project_kernel, grid_spec=pltpu.PrefetchScalarGridSpec(num...  14.1 us
    ppermute x4, waiting for transfers between devices, from_behind(): return lax.ppermute(block, axis, route)  13.7 us
  transfers between devices with their start and end apart: 6, of which 2 were waited for; matrix products, arithmetic and copies ran while one was open for 3% of the time, Pallas kernels for 24%

profile of v1, /device:TPU:1, one launch (start us, length us, event | category | flops | bytes accessed | tf_op | source)
XLA Modules:
  0.0 201.1 jit_solution(17271305094179124085)
XLA Ops:
  1.3 9.9 %collective-permute-start.2 = (s32[1]{0:T(128)}, s32[1]{0:T(128)}, u32[]{:S(2)}, u32[]{:S(2)}) collective-permute-start(s32[1]{0:T(128)} %add.24), channel_id=1, source_target_pairs={{1,0},{2,1},{3,2},{4,3},{5,4},{6,5},{7,6},{8,7},{9,8},{10,9},{11,1... | collective-permute-start | bytes 20 | tf_op jit(solution)/shard_map/ppermute | solution.py:29
  11.2 1.0 slice.16
  12.2 3.3 %collective-permute-start.1 = (bf16[64,2048]{1,0:T(8,128)(2,1)S(1)}, bf16[64,2048]{1,0:T(8,128)(2,1)S(1)}, u32[]{:S(2)}, u32[]{:S(2)}) collective-permute-start(bf16[64,2048]{1,0:T(8,128)(2,1)S(1)} %slice.16), channel_id=1, source_target_pairs={{1,0},{2,1},{3,2},{4,3},{5,4},{6,5},{7,6},{8,7},{9,8},{10,9},{11,1... | collective-permute-start | bytes 786440 | tf_op jit(solution)/shard_map/ppermute | solution.py:29
  15.5 1.0 slice.15
  16.5 2.4 %collective-permute-start = (bf16[64,2048]{1,0:T(8,128)(2,1)S(1)}, bf16[64,2048]{1,0:T(8,128)(2,1)S(1)}, u32[]{:S(2)}, u32[]{:S(2)}) collective-permute-start(bf16[64,2048]{1,0:T(8,128)(2,1)S(1)} %slice.15), channel_id=1, source_target_pairs={{1,0},{2,1},{3,2},{4,3},{5,4},{6,5},{7,6},{8,7},{9,8},{10,9},{11,1... | collective-permute-start | bytes 786440 | tf_op jit(solution)/shard_map/ppermute | solution.py:29
  19.6 0.8 copy.13
  21.1 15.3 %encode.1 = bf16[16,9,8,896]{3,2,1,0:T(8,128)(2,1)} custom-call(bf16[8,128,896]{2,1,0:T(8,128)(2,1)} %tok_ref.1, bf16[8,896]{1,0:T(8,128)(2,1)} %pad.4.ids_ref, bf16[896,1792]{1,0:T(8,128)(2,1)} %win_ref.1, bf16[1792,896]{1,0:T(8,128)(2,1)} %wout_ref.1), custom_call_target="tpu_custom_call" | custom-call | tf_op jit(solution)/shard_map/encode/pallas_call | solution.py:70
  36.4 1.3 compare_convert_fusion.valid_ref
  37.7 3.7 %all-to-all-start = ((bf16[16,9,8,896]{3,2,1,0:T(8,128)(2,1)}), bf16[16,9,8,896]{3,2,1,0:T(8,128)(2,1)S(1)}, u32[]{:S(2)}, u32[]{:S(2)}) async-start(bf16[16,9,8,896]{3,2,1,0:T(8,128)(2,1)} %encode.1), calls=%async_computation | async-start | bytes 4128768 | tf_op jit(solution)/shard_map/all_to_all | solution.py:33
  41.5 14.1 %project.1 = (bf16[4,16,64,896]{3,2,1,0:T(8,128)(2,1)}, bf16[4,16,64,896]{3,2,1,0:T(8,128)(2,1)}) custom-call(s32[4]{0:T(128)} %compare_convert_fusion.valid_ref, bf16[256,2048]{1,0:T(8,128)(2,1)} %q_ref.1, bf16[64,2048]{1,0:T(8,128)(2,1)} %copy-done.3, bf16[256,2048]{1,0:T(8,128)(2,1)} %g_ref.1, bf16[64,2048]{1,0:T(8,128)(2,1)} %copy-done.2, ...), custom_call_target="tpu_custom_call" | custom-call | tf_op jit(solution)/shard_map/project/pallas_call | solution.py:187
  55.6 17.4 %all-to-all-done.refs_1_ = bf16[16,9,8,896]{3,2,1,0:T(8,128)(2,1)S(1)} async-done(((bf16[16,9,8,896]{3,2,1,0:T(8,128)(2,1)}), bf16[16,9,8,896]{3,2,1,0:T(8,128)(2,1)S(1)}, u32[]{:S(2)}, u32[]{:S(2)}) %all-to-all-start) | async-done | bytes 2064416 | tf_op jit(solution)/shard_map/all_to_all | solution.py:33
  73.0 0.7 reshape.96.refs_0_
  74.2 4.4 %reorder.1 = bf16[16,8,8,896]{3,2,1,0:T(8,128)(2,1)} custom-call(s32[128]{0:T(128)} %reshape.96.refs_0_, bf16[16,9,8,896]{3,2,1,0:T(8,128)(2,1)} %copy-done), custom_call_target="tpu_custom_call" | custom-call | tf_op jit(solution)/shard_map/reorder/pallas_call | solution.py:106
  78.7 28.4 %all_to_all.20 = bf16[16,8,8,896]{3,2,1,0:T(8,128)(2,1)} all-to-all(bf16[16,8,8,896]{3,2,1,0:T(8,128)(2,1)} %reorder.1), channel_id=1, replica_groups=mesh['seq'=8,'nbr'=16] {'nbr'}, dimensions={0} | all-to-all | bytes 3670016 | tf_op jit(solution)/shard_map/all_to_all | solution.py:33
  107.1 16.7 %attend.1 = (bf16[16,4,16,896]{3,2,1,0:T(8,128)(2,1)}, bf16[4,256,1024]{2,1,0:T(8,128)(2,1)}) custom-call(bf16[16,4,16,896]{3,2,1,0:T(8,128)(2,1)} %bitcast.6, bf16[4,1024,896]{2,1,0:T(8,128)(2,1)} %bitcast.8, bf16[4,1024,896]{2,1,0:T(8,128)(2,1)} %bitcast.9), custom_call_target="tpu_custom_call" | custom-call | tf_op jit(solution)/shard_map/attend/pallas_call | solution.py:231
  123.8 27.8 %all_to_all.21.refs_1_ = bf16[16,8,8,896]{3,2,1,0:T(8,128)(2,1)} all-to-all(bf16[16,8,8,896]{3,2,1,0:T(8,128)(2,1)} %bitcast.11), channel_id=1, replica_groups=mesh['seq'=8,'nbr'=16] {'nbr'}, dimensions={0} | all-to-all | bytes 3670016 | tf_op jit(solution)/shard_map/all_to_all | solution.py:33
  151.6 4.3 %reorder_back.1 = bf16[16,8,8,896]{3,2,1,0:T(8,128)(2,1)} custom-call(s32[128]{0:T(128)} %reshape.96.refs_0_, bf16[16,8,8,896]{3,2,1,0:T(8,128)(2,1)} %all_to_all.21.refs_1_), custom_call_target="tpu_custom_call" | custom-call | tf_op jit(solution)/shard_map/reorder_back/pallas_call | solution.py:106
  156.0 3.7 %all-to-all-start.3 = ((bf16[16,8,8,896]{3,2,1,0:T(8,128)(2,1)}), bf16[16,8,8,896]{3,2,1,0:T(8,128)(2,1)S(1)}, u32[]{:S(2)}, u32[]{:S(2)}) async-start(bf16[16,8,8,896]{3,2,1,0:T(8,128)(2,1)} %reorder_back.1), calls=%async_computation.3 | async-start | bytes 3670016 | tf_op jit(solution)/shard_map/all_to_all | solution.py:33
  159.7 18.0 %mix.1 = (bf16[256,2048]{1,0:T(8,128)(2,1)}, bf16[64,2048]{1,0:T(8,128)(2,1)}) custom-call(s32[4]{0:T(128)} %compare_convert_fusion.valid_ref, bf16[16,4,16,896]{3,2,1,0:T(8,128)(2,1)} %bitcast.7, bf16[4,256,1024]{2,1,0:T(8,128)(2,1)} %get-tuple-element.26.weight_ref, bf16[896,2048]{1,0:T(8,128)(2,1)} %wv_ref.3), custom_call_target="tpu_custom_call" | custom-call | tf_op jit(solution)/shard_map/mix/pallas_call | solution.py:271
  177.7 3.1 %collective-permute-start.3 = (bf16[64,2048]{1,0:T(8,128)(2,1)}, bf16[64,2048]{1,0:T(8,128)(2,1)S(1)}, u32[]{:S(2)}, u32[]{:S(2)}) collective-permute-start(bf16[64,2048]{1,0:T(8,128)(2,1)} %get-tuple-element.28), channel_id=1, source_target_pairs={{0,1},{1,2},{2,3},{3,4},{4,5},{5,6},{6,7},{7,8},{8,9},{9,10},{10,1... | collective-permute-start | bytes 786440 | tf_op jit(solution)/shard_map/ppermute | solution.py:29
  180.9 13.7 %collective-permute-done.3.carried_ref = bf16[64,2048]{1,0:T(8,128)(2,1)S(1)} collective-permute-done((bf16[64,2048]{1,0:T(8,128)(2,1)}, bf16[64,2048]{1,0:T(8,128)(2,1)S(1)}, u32[]{:S(2)}, u32[]{:S(2)}) %collective-permute-start.3) | collective-permute-done | bytes 262176 | tf_op jit(solution)/shard_map/ppermute | solution.py:29
  195.3 1.8 join.1
  197.1 1.3 copy-done.1
  198.3 2.8 %regroup.1 = bf16[8,16,8,896]{3,2,1,0:T(8,128)(2,1)} custom-call(bf16[16,8,8,896]{3,2,1,0:T(8,128)(2,1)} %copy-done.1), custom_call_target="tpu_custom_call" | custom-call | tf_op jit(solution)/shard_map/regroup/pallas_call | solution.py:133
  (21 shorter events, 2.7 us)
Async XLA Ops:
  1.3 35.1 %collective-permute-start.2 = (s32[1]{0:T(128)}, s32[1]{0:T(128)}, u32[]{:S(2)}, u32[]{:S(2)}) collective-permute-start(s32[1]{0:T(128)} %add.24), channel_id=1, source_target_pairs={{1,0},{2,1},{3,2},{4,3},{5,4},{6,5},{7,6},{8,7},{9,8},{10,9},{11,1... | collective-permute-start | bytes 20 | tf_op jit(solution)/shard_map/ppermute | solution.py:29
  12.2 25.5 %collective-permute-start.1 = (bf16[64,2048]{1,0:T(8,128)(2,1)S(1)}, bf16[64,2048]{1,0:T(8,128)(2,1)S(1)}, u32[]{:S(2)}, u32[]{:S(2)}) collective-permute-start(bf16[64,2048]{1,0:T(8,128)(2,1)S(1)} %slice.16), channel_id=1, source_target_pairs={{1,0},{2,1},{3,2},{4,3},{5,4},{6,5},{7,6},{8,7},{9,8},{10,9},{11,1... | collective-permute-start | bytes 786440 | tf_op jit(solution)/shard_map/ppermute | solution.py:29
  16.5 21.2 %collective-permute-start = (bf16[64,2048]{1,0:T(8,128)(2,1)S(1)}, bf16[64,2048]{1,0:T(8,128)(2,1)S(1)}, u32[]{:S(2)}, u32[]{:S(2)}) collective-permute-start(bf16[64,2048]{1,0:T(8,128)(2,1)S(1)} %slice.15), channel_id=1, source_target_pairs={{1,0},{2,1},{3,2},{4,3},{5,4},{6,5},{7,6},{8,7},{9,8},{10,9},{11,1... | collective-permute-start | bytes 786440 | tf_op jit(solution)/shard_map/ppermute | solution.py:29
  21.1 15.3 %copy-start.5 = (s32[4]{0:T(128)S(1)}, s32[4]{0:T(128)}, u32[]{:S(2)}) copy-start(s32[4]{0:T(128)} %param.14) | copy-start | bytes 52
  37.7 3.8 %copy-start.2 = (bf16[64,2048]{1,0:T(8,128)(2,1)}, bf16[64,2048]{1,0:T(8,128)(2,1)S(1)}, u32[]{:S(2)}) copy-start(bf16[64,2048]{1,0:T(8,128)(2,1)S(1)} %collective-permute-done.1.ng_ref) | copy-start | bytes 786436
  37.7 3.8 %copy-start.3 = (bf16[64,2048]{1,0:T(8,128)(2,1)}, bf16[64,2048]{1,0:T(8,128)(2,1)S(1)}, u32[]{:S(2)}) copy-start(bf16[64,2048]{1,0:T(8,128)(2,1)S(1)} %collective-permute-done.nq_ref) | copy-start | bytes 786436
  37.7 35.2 %all-to-all-start = ((bf16[16,9,8,896]{3,2,1,0:T(8,128)(2,1)}), bf16[16,9,8,896]{3,2,1,0:T(8,128)(2,1)S(1)}, u32[]{:S(2)}, u32[]{:S(2)}) async-start(bf16[16,9,8,896]{3,2,1,0:T(8,128)(2,1)} %encode.1), calls=%async_computation | async-start | bytes 4128768 | tf_op jit(solution)/shard_map/all_to_all | solution.py:33
  72.9 1.3 copy-start
  156.0 41.1 %all-to-all-start.3 = ((bf16[16,8,8,896]{3,2,1,0:T(8,128)(2,1)}), bf16[16,8,8,896]{3,2,1,0:T(8,128)(2,1)S(1)}, u32[]{:S(2)}, u32[]{:S(2)}) async-start(bf16[16,8,8,896]{3,2,1,0:T(8,128)(2,1)} %reorder_back.1), calls=%async_computation.3 | async-start | bytes 3670016 | tf_op jit(solution)/shard_map/all_to_all | solution.py:33
  177.7 16.9 %collective-permute-start.3 = (bf16[64,2048]{1,0:T(8,128)(2,1)}, bf16[64,2048]{1,0:T(8,128)(2,1)S(1)}, u32[]{:S(2)}, u32[]{:S(2)}) collective-permute-start(bf16[64,2048]{1,0:T(8,128)(2,1)} %get-tuple-element.28), channel_id=1, source_target_pairs={{0,1},{1,2},{2,3},{3,4},{4,5},{5,6},{6,7},{7,8},{8,9},{9,10},{10,1... | collective-permute-start | bytes 786440 | tf_op jit(solution)/shard_map/ppermute | solution.py:29
  194.6 0.7 copy-start.4
  197.1 1.3 copy-start.1

commit v2 on v1

v2 whole, which is shorter than its diff:
```python
import math

import jax
import jax.numpy as jnp
from jax import lax
from jax.experimental import pallas as pl
from jax.experimental.pallas import tpu as pltpu
from jax.sharding import PartitionSpec as P

HEAD = 128
EPS = 1e-06
PIECE = 8
NT = (((1,), (1,)), ((), ()))
TN = (((0,), (0,)), ((), ()))
F32 = jnp.float32
BF16 = jnp.bfloat16
VMEM_LIMIT = 32 * 1024 * 1024


def params(n=1):
    return pltpu.CompilerParams(
        dimension_semantics=("arbitrary",) * n, vmem_limit_bytes=VMEM_LIMIT
    )


def from_behind(block, axis, distance):
    devices = range(lax.axis_size(axis))
    route = [(i - distance, i) for i in devices if i - distance in devices]
    return lax.ppermute(block, axis, route)


def spread(block):
    return lax.all_to_all(block, "nbr", split_axis=0, concat_axis=0, tiled=True)


def in_vmem(block):
    return pltpu.with_memory_space_constraint(block, pltpu.VMEM)


def in_hbm(block):
    return pltpu.with_memory_space_constraint(block, pltpu.HBM)


def encode_kernel(ids_ref, tok, win, wout_hbm, out_ref, wout, normed, hid, stage, sems):
    count, length, width = tok.shape
    pieces = length // PIECE
    items = count // 2
    rows = items * length
    chunk = 256
    wout_copy = pltpu.make_async_copy(wout_hbm, wout, sems.at[0])
    wout_copy.start()

    row = lax.broadcasted_iota(jnp.int32, (PIECE, width), 0)
    own = jnp.zeros((PIECE, width), jnp.int32)
    for r in range(count):
        own = jnp.where(row == r, ids_ref[r % 2, r // 2] % (pieces * count), own)
    own = own.astype(F32).astype(BF16)
    for p in range(pieces):
        stage[p, count] = own

    def norm(b):
        x = tok[pl.ds(b * items, items)].reshape(rows, width).astype(F32)
        scale = lax.rsqrt(jnp.mean(x * x, axis=-1, keepdims=True) + EPS)
        normed[b] = (x * scale).astype(BF16)

    outs = []
    norm(0)
    for b in range(2):
        for f in range(win.shape[1] // chunk):
            at = slice(f * chunk, (f + 1) * chunk)
            hidden = jnp.dot(normed[b], win[:, at], preferred_element_type=F32)
            hid[b, :, at] = jax.nn.gelu(hidden, approximate=True).astype(BF16)
        if b == 0:
            norm(1)
            wout_copy.wait()
        y = jnp.dot(hid[b], wout[...], preferred_element_type=F32)
        y = (y + tok[pl.ds(b * items, items)].reshape(rows, width).astype(F32)).astype(BF16)
        for i in range(items):
            stage[:, b * items + i] = y[i * length : (i + 1) * length].reshape(pieces, PIECE, width)
        part = pl.ds(b * items, items + b)
        outs.append(pltpu.make_async_copy(stage.at[:, part], out_ref.at[:, part], sems.at[1 + b]))
        outs[b].start()
    for copy in outs:
        copy.wait()


def encode(tokens, ids, enc_in, enc_out):
    count, length, width = tokens.shape
    hidden = enc_in.shape[1]
    shape = (length // PIECE, count + 1, PIECE, width)
    rows = count // 2 * length
    inside = pl.BlockSpec(memory_space=pltpu.VMEM)
    anywhere = pl.BlockSpec(memory_space=pltpu.HBM)
    return pl.pallas_call(
        encode_kernel,
        in_specs=[pl.BlockSpec(memory_space=pltpu.SMEM), inside, inside, anywhere],
        out_specs=anywhere,
        out_shape=pltpu.HBM(shape, BF16),
        scratch_shapes=[
            pltpu.VMEM(enc_out.shape, BF16),
            pltpu.VMEM((2, rows, width), BF16),
            pltpu.VMEM((2, rows, hidden), BF16),
            pltpu.VMEM(shape, BF16),
            pltpu.SemaphoreType.DMA((3,)),
        ],
        compiler_params=pltpu.CompilerParams(vmem_limit_bytes=32 << 20),
        name="encode",
    )(ids.T, in_vmem(tokens), in_vmem(enc_in), in_hbm(enc_out))


def reorder_kernel(inverse, table_ref, src_ref, dst_ref, sem):
    peers, count = dst_ref.shape[:2]
    for j in range(peers):
        for k in range(count):
            at = table_ref[j * count + k]
            there = (at // count, at % count)
            a, b = ((j, k), there) if inverse else (there, (j, k))
            pltpu.make_async_copy(src_ref.at[a[0], a[1]], dst_ref.at[b[0], b[1]], sem).start()
    pltpu.make_async_copy(src_ref.at[:, pl.ds(0, count)], dst_ref, sem).wait()


def reorder(table, block, count, inverse):
    return pl.pallas_call(
        lambda *refs: reorder_kernel(inverse, *refs),
        grid_spec=pltpu.PrefetchScalarGridSpec(
            num_scalar_prefetch=1,
            in_specs=[pl.BlockSpec(memory_space=pltpu.VMEM)],
            out_specs=pl.BlockSpec(memory_space=pltpu.HBM),
            scratch_shapes=[pltpu.SemaphoreType.DMA],
        ),
        out_shape=pltpu.HBM(block.shape[:1] + (count,) + block.shape[2:], block.dtype),
        compiler_params=pltpu.CompilerParams(vmem_limit_bytes=4 << 20),
        name="reorder_back" if inverse else "reorder",
    )(table, in_vmem(block))


def regroup_kernel(src_ref, dst_ref, sem):
    copies = [
        pltpu.make_async_copy(src_ref.at[:, i], dst_ref.at[i], sem.at[i])
        for i in range(dst_ref.shape[0])
    ]
    for copy in copies:
        copy.start()
    for copy in copies:
        copy.wait()


def regroup(block):
    pieces, count, rows, width = block.shape
    out = pl.pallas_call(
        regroup_kernel,
        in_specs=[pl.BlockSpec(memory_space=pltpu.VMEM)],
        out_specs=pl.BlockSpec(memory_space=pltpu.HBM),
        out_shape=jax.ShapeDtypeStruct((count, pieces, rows, width), block.dtype),
        scratch_shapes=[pltpu.SemaphoreType.DMA((count,))],
        compiler_params=pltpu.CompilerParams(vmem_limit_bytes=4 << 20),
        name="regroup",
    )(in_vmem(block))
    return out.reshape(count, pieces * rows, width)


def pack_kernel(label_ref, q_ref, g_ref, tok_hbm, win_hbm, out_ref, tok_ref, win_ref, q, g, sems):
    span = q.shape[0]
    copies = [
        pltpu.make_async_copy(q_ref.at[pl.ds(0, span)], q, sems.at[0]),
        pltpu.make_async_copy(g_ref.at[pl.ds(0, span)], g, sems.at[1]),
        pltpu.make_async_copy(tok_hbm, tok_ref, sems.at[2]),
        pltpu.make_async_copy(win_hbm, win_ref, sems.at[3]),
    ]
    for copy in copies:
        copy.start()
    for copy in copies[:2]:
        copy.wait()
    last = lax.broadcasted_iota(jnp.int32, q.shape, 0) == span - 1
    label = (label_ref[0] + 1).astype(F32)
    out_ref[0] = jnp.where(last, label, q[...].astype(F32)).astype(BF16)
    out_ref[1] = g[...]
    for copy in copies[2:]:
        copy.wait()


def pack(sequence_ids, queries, cotangent, tokens, enc_in, span):
    features = queries.shape[1]
    inside = pl.BlockSpec(memory_space=pltpu.VMEM)
    anywhere = pl.BlockSpec(memory_space=pltpu.HBM)
    return pl.pallas_call(
        pack_kernel,
        in_specs=[pl.BlockSpec(memory_space=pltpu.SMEM)] + [anywhere] * 4,
        out_specs=[inside] * 3,
        out_shape=[
            pltpu.VMEM((2, span, features), BF16),
            pltpu.VMEM(tokens.shape, BF16),
            pltpu.VMEM(enc_in.shape, BF16),
        ],
        scratch_shapes=[
            pltpu.VMEM((span, features), BF16),
            pltpu.VMEM((span, features), BF16),
            pltpu.SemaphoreType.DMA((4,)),
        ],
        compiler_params=pltpu.CompilerParams(vmem_limit_bytes=16 << 20),
        name="pack",
    )(sequence_ids, in_hbm(queries), in_hbm(cotangent), in_hbm(tokens), in_hbm(enc_in))


def span_rows(own, later, span):
    last = lax.broadcasted_iota(jnp.int32, (span, own.shape[1]), 0) == span - 1
    blocks = own.shape[0] // span
    out = []
    for c in range(blocks):
        here = own[c * span : (c + 1) * span]
        after = own[(c + 1) * span : (c + 2) * span] if c + 1 < blocks else later
        out.append(jnp.where(last, here, after))
    return out


def row_valid(valid_ref, c, span, width):
    last = lax.broadcasted_iota(jnp.int32, (span, width), 0) == span - 1
    return jnp.where(last, 1.0, valid_ref[c].astype(F32))


def project_kernel(valid_ref, q_ref, g_ref, next_ref, wk_ref, wv_ref, out_ref):
    spans, _, heads, span, width = out_ref.shape
    inv_root = 1.0 / math.sqrt(HEAD)
    q = span_rows(q_ref[...].astype(F32), next_ref[0].astype(F32), span)
    g = span_rows(g_ref[...].astype(F32), next_ref[1].astype(F32), span)
    g = [g[c] * row_valid(valid_ref, c, span, g[c].shape[1]) for c in range(spans)]
    q = jnp.concatenate(q, 0).astype(BF16)
    g = jnp.concatenate(g, 0).astype(BF16)
    for h in range(heads):
        at = slice(h * HEAD, (h + 1) * HEAD)
        qw = lax.dot_general(q[:, at], wk_ref[:, at], NT, preferred_element_type=F32)
        out_ref[:, 0, h] = (qw * inv_root).astype(BF16).reshape(spans, span, width)
        mw = lax.dot_general(g[:, at], wv_ref[:, at], NT, preferred_element_type=F32)
        out_ref[:, 1, h] = mw.astype(BF16).reshape(spans, span, width)


def project(valid, queries, cotangent, next_rows, key_weight, value_weight, span):
    rows, features = queries.shape
    width = key_weight.shape[0]
    spans = rows // span
    heads = 2
    block = heads * HEAD
    tall = pl.BlockSpec((rows, block), lambda f, v: (0, f))
    short = pl.BlockSpec((2, span, block), lambda f, v: (0, 0, f))
    wide = pl.BlockSpec((width, block), lambda f, v: (0, f))
    out = pl.BlockSpec((spans, 2, heads, span, width), lambda f, v: (0, 0, f, 0, 0))
    shape = pltpu.HBM((spans, 2, features // HEAD, span, width), BF16)
    return pl.pallas_call(
        project_kernel,
        grid_spec=pltpu.PrefetchScalarGridSpec(
            num_scalar_prefetch=1,
            grid=(features // block,),
            in_specs=[tall, tall, short, wide, wide],
            out_specs=out,
        ),
        out_shape=shape,
        compiler_params=pltpu.CompilerParams(
            dimension_semantics=("arbitrary",), vmem_limit_bytes=16 << 20
        ),
        name="project",
    )(valid, queries, cotangent, next_rows, key_weight, value_weight)


def attend_kernel(
    x_ref, proj_hbm, grad_ref, weight_ref, proj_ref, shares_out, grads_out, scored, sems, proj_sems
):
    pieces, spans, rows, width = x_ref.shape
    columns = proj_ref.shape[2]
    block = 256

    def arrival(c, b):
        at = pl.ds(b * columns // 2, columns // 2)
        return pltpu.make_async_copy(
            proj_hbm.at[c, :, at], proj_ref.at[c, :, at], proj_sems.at[c, b]
        )

    arrival(0, 0).start()
    arrival(0, 1).start()

    def span(c):
        x = x_ref[:, c].reshape(pieces * rows, width)

        def products(b):
            if b == 0:
                arrival(c, 0).wait()
                if c + 1 < spans:
                    arrival(c + 1, 0).start()
                    arrival(c + 1, 1).start()
                if c > 0:
                    arrival(c, 1).wait()
            if c == 0 and b == columns // block // 2:
                arrival(0, 1).wait()
            at = slice(b * block, (b + 1) * block)
            return (
                lax.dot_general(x, proj_ref[c, 0, at, :], NT, preferred_element_type=F32),
                lax.dot_general(x, proj_ref[c, 1, at, :], NT, preferred_element_type=F32),
            )

        later = products(0)
        for b in range(columns // block):
            scores, grad_weights = later
            if (b + 1) * block < columns:
                later = products(b + 1)
            at = slice(b * block, (b + 1) * block)
            shares = jnp.exp(scores - jnp.max(scores, axis=0, keepdims=True))
            shares = shares * (1.0 / jnp.sum(shares, axis=0, keepdims=True))
            inner = jnp.sum(shares * grad_weights, axis=0, keepdims=True)
            shares_out[c, :, at] = shares.astype(BF16)
            scored[c % 2, :, at] = (shares * (grad_weights - inner)).astype(BF16)

    copies = []

    def finish(c):
        total = jnp.dot(scored[c % 2], proj_ref[c, 0], preferred_element_type=F32)
        total += jnp.dot(shares_out[c], proj_ref[c, 1], preferred_element_type=F32)
        grads_out[c] = total.astype(BF16).reshape(pieces, rows, width)
        copies.append(pltpu.make_async_copy(grads_out.at[c], grad_ref.at[:, c], sems.at[0, c]))
        copies[-1].start()

    for c in range(spans + 1):
        if c < spans:
            span(c)
            copies.append(pltpu.make_async_copy(shares_out.at[c], weight_ref.at[c], sems.at[1, c]))
            copies[-1].start()
        if c > 0:
            finish(c - 1)
    for copy in copies:
        copy.wait()


def attend(slots, projected):
    pieces, spans, rows, width = slots.shape
    columns = projected.shape[2]
    shares = (spans, pieces * rows, columns)
    inside = pl.BlockSpec(memory_space=pltpu.VMEM)
    anywhere = pl.BlockSpec(memory_space=pltpu.HBM)
    return pl.pallas_call(
        attend_kernel,
        in_specs=[inside, anywhere],
        out_specs=[anywhere] * 2,
        out_shape=[pltpu.HBM(slots.shape, BF16), pltpu.HBM(shares, BF16)],
        scratch_shapes=[
            pltpu.VMEM(projected.shape, BF16),
            pltpu.VMEM(shares, BF16),
            pltpu.VMEM((spans, pieces, rows, width), BF16),
            pltpu.VMEM((2,) + shares[1:], BF16),
            pltpu.SemaphoreType.DMA((2, spans)),
            pltpu.SemaphoreType.DMA((spans, 2)),
        ],
        compiler_params=pltpu.CompilerParams(vmem_limit_bytes=40 << 20),
        name="attend",
    )(in_vmem(slots), in_hbm(projected))


def mix_kernel(valid_ref, x_ref, weight_ref, wv_ref, out_ref, tail_ref, before):
    c = pl.program_id(0)
    pieces, _, rows, width = x_ref.shape
    span = out_ref.shape[0]
    x = x_ref[:, 0].reshape(pieces * rows, width)
    pair = 2 * HEAD
    scale = row_valid(valid_ref, c, span, HEAD)
    last = lax.broadcasted_iota(jnp.int32, (span, HEAD), 0) == span - 1
    for b in range(wv_ref.shape[1] // pair):
        values = jnp.dot(x, wv_ref[:, b * pair : (b + 1) * pair], preferred_element_type=F32)
        weights = weight_ref[0, :, b * 2 * span : (b + 1) * 2 * span]
        mixed = lax.dot_general(weights, values.astype(BF16), TN, preferred_element_type=F32)
        for h in range(2):
            at = slice(b * pair + h * HEAD, b * pair + (h + 1) * HEAD)
            now = mixed[h * span : (h + 1) * span, h * HEAD : (h + 1) * HEAD] * scale
            out_ref[:, at] = jnp.where(last, now, before[:, at]).astype(BF16)
            before[:, at] = now

    @pl.when(c == pl.num_programs(0) - 1)
    def _():
        tail_ref[...] = before[...].astype(BF16)


def mix(valid, slots, weights, value_weight, span):
    pieces, spans, rows, width = slots.shape
    features = value_weight.shape[1]
    return pl.pallas_call(
        mix_kernel,
        grid_spec=pltpu.PrefetchScalarGridSpec(
            num_scalar_prefetch=1,
            grid=(spans,),
            in_specs=[
                pl.BlockSpec((pieces, 1, rows, width), lambda c, v: (0, c, 0, 0)),
                pl.BlockSpec((1,) + weights.shape[1:], lambda c, v: (c, 0, 0)),
                pl.BlockSpec((width, features), lambda c, v: (0, 0)),
            ],
            out_specs=[
                pl.BlockSpec((span, features), lambda c, v: (c, 0)),
                pl.BlockSpec((span, features), lambda c, v: (0, 0)),
            ],
            scratch_shapes=[pltpu.VMEM((span, features), F32)],
        ),
        out_shape=[
            jax.ShapeDtypeStruct((spans * span, features), BF16),
            jax.ShapeDtypeStruct((span, features), BF16),
        ],
        compiler_params=params(),
        name="mix",
    )(valid, slots, weights, value_weight)


def join_kernel(whole_ref, carried_ref, out_ref):
    span, features = out_ref.shape
    last = lax.broadcasted_iota(jnp.int32, (span, features), 0) == span - 1
    out_ref[...] = jnp.where(
        last, whole_ref[...].astype(F32), carried_ref[...].astype(F32)
    ).astype(BF16)


def join(whole, carried):
    first = pl.BlockSpec(carried.shape, lambda i: (0, 0))
    return pl.pallas_call(
        join_kernel,
        grid=(1,),
        in_specs=[first, first],
        out_specs=first,
        out_shape=jax.ShapeDtypeStruct(whole.shape, whole.dtype),
        input_output_aliases={0: 0},
        compiler_params=params(),
        name="join",
    )(whole, carried)


def shards(
    queries,
    cotangent,
    neighbour_tokens,
    neighbour_ids,
    neighbour_dest,
    sequence_ids,
    enc_in,
    enc_out,
    key_weight,
    value_weight,
):
    spans = sequence_ids.shape[0]
    rows, features = queries.shape
    span = rows // spans
    count, length, width = neighbour_tokens.shape
    peers = lax.axis_size("nbr")
    everyone = ("seq", "nbr")

    first_rows, tokens, up = pack(
        sequence_ids, queries, cotangent, neighbour_tokens, enc_in, span
    )
    next_rows = from_behind(first_rows, everyone, -1)
    pieces = encode(tokens, neighbour_ids, up, enc_out)
    pieces, next_rows = lax.optimization_barrier((pieces, next_rows))
    held = spread(pieces)
    labels = (sequence_ids + 1).astype(BF16)
    next_label = next_rows[0, span - 1, :1]
    valid = (labels == jnp.concatenate([labels[1:], next_label], 0)).astype(jnp.int32)
    table = held[:, count, :, 0].astype(jnp.int32).reshape(-1)
    projected = project(valid, queries, cotangent, next_rows, key_weight, value_weight, span)
    held, table, projected = lax.optimization_barrier((held, table, projected))
    slots = spread(reorder(table, held, count, False))
    pair = (peers, spans, count // spans * PIECE, width)
    columns = features // HEAD * span
    grads, weights = attend(slots.reshape(pair), projected.reshape(spans, 2, columns, width))
    held_grads = spread(grads.reshape(slots.shape))
    whole, tail = mix(valid, slots.reshape(pair), weights, value_weight, span)
    held_grads, whole, tail = lax.optimization_barrier((held_grads, whole, tail))
    carried = from_behind(tail, everyone, 1)
    attended = join(whole, carried)
    returned = spread(reorder(table, held_grads, count, True))
    return attended, regroup(returned)


def solution(mesh):
    rows = P(("seq", "nbr"), None)
    blocks = P(("seq", "nbr"), None, None)
    flat = P(("seq", "nbr"))
    in_specs = (rows, rows, blocks, rows, flat, flat, P(), P(), P(), P())
    return jax.shard_map(
        shards, mesh=mesh, in_specs=in_specs, out_specs=(rows, blocks), check_vma=False
    )
```

time: 202 us -> 187 us (0.926)
  blocking collectives: 56.3 us -> 30.8 us
  waiting for transfers between devices: 31.1 us -> 51.3 us
  Pallas kernels: 77.4 us -> 61.7 us
  local copies, waits for them, and re-layouts: 6.71 us -> 10.9 us
  starting transfers between devices: 26.3 us -> 29.1 us
    all_to_all x2 -> x1, blocking collectives: 56.3 us -> 30.8 us  [spread(): return lax.all_to_all(block, 'nbr', split_axis=0, concat_axis=0, tiled=True)]
    ppermute x4 -> x2, waiting for transfers between devices: 13.7 us -> 29.3 us  [from_behind(): return lax.ppermute(block, axis, route)]
    all_to_all x2 -> x3, starting transfers between devices: 7.46 us -> 16.7 us  [spread(): return lax.all_to_all(block, 'nbr', split_axis=0, concat_axis=0, tiled=True)]
    ppermute x4 -> x2, starting transfers between devices: 18.8 us -> 12.4 us  [from_behind(): return lax.ppermute(block, axis, route)]
    unnamed x13 -> x18, local copies, waits for them, and re-layouts: 3.29 us -> 9.59 us
    pallas_call x2 -> x3, Pallas kernels: 31.9 us -> 27.2 us  [the longest x1 13.2 us: attend(): pl.pallas_call(attend_kernel, in_specs=[inside, anywhere], out_specs=[any...]
    all_to_all x2 -> x3, waiting for transfers between devices: 17.4 us -> 21.9 us  [spread(): return lax.all_to_all(block, 'nbr', split_axis=0, concat_axis=0, tiled=True)]
    pallas_call x1, Pallas kernels: 14.1 us -> 10.3 us  [project(): pl.pallas_call(project_kernel, grid_spec=pltpu.PrefetchScalarGridSpec(num...]
  transfers between devices with their start and end apart: 6 -> 5, of which waited for: 2 -> 3; matrix products, arithmetic and copies ran while one was open for 3% -> 1% of each run, Pallas kernels for 24% -> 21%
where the time goes in v2:
time: 187 us; the launch traced here: 186 us
  Pallas kernels  61.7 us (33%)
  waiting for transfers between devices  51.3 us (27%)
  blocking collectives  30.8 us (16%)
  starting transfers between devices  29.1 us (16%)
  local copies, waits for them, and re-layouts  10.9 us (6%)
    all_to_all x1, blocking collectives, spread(): return lax.all_to_all(block, 'nbr', split_axis=0, concat_axis=0, tiled=True)  30.8 us
    ppermute x2, waiting for transfers between devices, from_behind(): return lax.ppermute(block, axis, route)  29.3 us
    all_to_all x3, waiting for transfers between devices, spread(): return lax.all_to_all(block, 'nbr', split_axis=0, concat_axis=0, tiled=True)  21.9 us
    all_to_all x3, starting transfers between devices, spread(): return lax.all_to_all(block, 'nbr', split_axis=0, concat_axis=0, tiled=True)  16.7 us
    pallas_call x1, Pallas kernels, mix(): pl.pallas_call(mix_kernel, grid_spec=pltpu.PrefetchScalarGridSpec(num_sca...  15.6 us
    pallas_call x1, Pallas kernels, attend(): pl.pallas_call(attend_kernel, in_specs=[inside, anywhere], out_specs=[any...  13.2 us
    ppermute x2, starting transfers between devices, from_behind(): return lax.ppermute(block, axis, route)  12.4 us
    pallas_call x1, Pallas kernels, encode(): pl.pallas_call(encode_kernel, in_specs=[pl.BlockSpec(memory_space=pltpu.S...  10.8 us
  transfers between devices with their start and end apart: 5, of which 3 were waited for; matrix products, arithmetic and copies ran while one was open for 1% of the time, Pallas kernels for 21%

profile of v2, /device:TPU:1, one launch (start us, length us, event | category | flops | bytes accessed | tf_op | source)
XLA Modules:
  0.0 185.8 jit_solution(18038096858626983090)
XLA Ops:
  1.3 3.2 %pack.1 = (bf16[2,64,2048]{2,1,0:T(8,128)(2,1)S(1)}, bf16[8,128,896]{2,1,0:T(8,128)(2,1)S(1)}, bf16[896,1792]{1,0:T(8,128)(2,1)S(1)}) custom-call(s32[4]{0:T(128)S(1)} %copy-done.6, bf16[256,2048]{1,0:T(8,128)(2,1)} %q_ref.3, bf16[256,2048]{1,0:T(8,128)(2,1)} %g_ref.3, bf16[8,128,896]{2,1,0:T(8,128)(2,1)} %tok_hbm.1, bf16[896,1792]{1,0:T(8,128)(2,1)} %win_hbm.1), custom_call_target="tpu_custom_call" | custom-call | tf_op jit(solution)/shard_map/pack/pallas_call | solution.py:186
  4.5 9.2 %collective-permute-start = (bf16[2,64,2048]{2,1,0:T(8,128)(2,1)S(1)}, bf16[2,64,2048]{2,1,0:T(8,128)(2,1)}, u32[]{:S(2)}, u32[]{:S(2)}) collective-permute-start(bf16[2,64,2048]{2,1,0:T(8,128)(2,1)S(1)} %get-tuple-element.19), channel_id=1, source_target_pairs={{1,0},{2,1},{3,2},{4,3},{5,4},{6,5},{7,6},{8,7},{9,8},{10,9},{11,1... | collective-permute-start | bytes 1572872 | tf_op jit(solution)/shard_map/ppermute | solution.py:29
  13.8 10.8 %encode.1 = bf16[16,9,8,896]{3,2,1,0:T(8,128)(2,1)} custom-call(s32[2,4]{1,0:T(2,128)S(1)} %bitcast.8, bf16[8,128,896]{2,1,0:T(8,128)(2,1)S(1)} %get-tuple-element.17.tok, bf16[896,1792]{1,0:T(8,128)(2,1)S(1)} %get-tuple-element.18.win, bf16[1792,896]{1,0:T(8,128)(2,1)} %wout_hbm.1), custom_call_target="tpu_custom_call" | custom-call | tf_op jit(solution)/shard_map/encode/pallas_call | solution.py:94
  24.6 8.4 %all-to-all-start = ((bf16[16,9,8,896]{3,2,1,0:T(8,128)(2,1)}), bf16[16,9,8,896]{3,2,1,0:T(8,128)(2,1)S(1)}, u32[]{:S(2)}, u32[]{:S(2)}) async-start(bf16[16,9,8,896]{3,2,1,0:T(8,128)(2,1)} %encode.1), calls=%async_computation | async-start | bytes 4128768 | tf_op jit(solution)/shard_map/all_to_all | solution.py:33
  33.1 1.2 slice.11
  35.0 2.0 %copy-done = bf16[896,2048]{1,0:T(8,128)(2,1)S(1)} copy-done((bf16[896,2048]{1,0:T(8,128)(2,1)S(1)}, bf16[896,2048]{1,0:T(8,128)(2,1)}, u32[]{:S(2)}) %copy-start) | copy-done | bytes 3670040
  37.1 1.2 copy-done.3
  38.3 2.0 %copy-done.4 = bf16[896,2048]{1,0:T(8,128)(2,1)S(1)} copy-done((bf16[896,2048]{1,0:T(8,128)(2,1)S(1)}, bf16[896,2048]{1,0:T(8,128)(2,1)}, u32[]{:S(2)}) %copy-start.4) | copy-done | bytes 3670040
  40.3 10.3 %project.1 = bf16[4,2,16,64,896]{4,3,2,1,0:T(8,128)(2,1)} custom-call(s32[4]{0:T(128)S(1)} %compare_convert_fusion.valid_ref, bf16[256,2048]{1,0:T(8,128)(2,1)S(1)} %copy-done.2, bf16[256,2048]{1,0:T(8,128)(2,1)S(1)} %copy-done.3, bf16[2,64,2048]{2,1,0:T(8,128)(2,1)} %collective-permute-done.next_ref, bf16[896,2048]{1,0:T(8,128)(2,1)S(1)} %copy-done.4, ...), custom_call_target="tpu_custom_call" | custom-call | tf_op jit(solution)/shard_map/project/pallas_call | solution.py:248
  50.6 12.8 %all-to-all-done.refs_1_ = bf16[16,9,8,896]{3,2,1,0:T(8,128)(2,1)S(1)} async-done(((bf16[16,9,8,896]{3,2,1,0:T(8,128)(2,1)}), bf16[16,9,8,896]{3,2,1,0:T(8,128)(2,1)S(1)}, u32[]{:S(2)}, u32[]{:S(2)}) %all-to-all-start) | async-done | bytes 2064416 | tf_op jit(solution)/shard_map/all_to_all | solution.py:33
  63.9 2.1 %reorder.1 = bf16[16,8,8,896]{3,2,1,0:T(8,128)(2,1)} custom-call(s32[128]{0:T(128)S(1)} %reshape.25.refs_0_, bf16[16,9,8,896]{3,2,1,0:T(8,128)(2,1)S(1)} %all-to-all-done.refs_1_), custom_call_target="tpu_custom_call" | custom-call | tf_op jit(solution)/shard_map/reorder/pallas_call | solution.py:123
  66.0 30.8 %all_to_all.20 = bf16[16,8,8,896]{3,2,1,0:T(8,128)(2,1)S(1)} all-to-all(bf16[16,8,8,896]{3,2,1,0:T(8,128)(2,1)} %reorder.1), channel_id=1, replica_groups=mesh['seq'=8,'nbr'=16] {'nbr'}, dimensions={0} | all-to-all | bytes 3670016 | tf_op jit(solution)/shard_map/all_to_all | solution.py:33
  96.8 13.2 %attend.1 = (bf16[16,4,16,896]{3,2,1,0:T(8,128)(2,1)}, bf16[4,256,1024]{2,1,0:T(8,128)(2,1)}) custom-call(bf16[16,4,16,896]{3,2,1,0:T(8,128)(2,1)S(1)} %bitcast.6, bf16[4,2,1024,896]{3,2,1,0:T(8,128)(2,1)} %bitcast.9), custom_call_target="tpu_custom_call" | custom-call | tf_op jit(solution)/shard_map/attend/pallas_call | solution.py:337
  110.0 4.7 %all-to-all-start.2 = ((bf16[16,8,8,896]{3,2,1,0:T(8,128)(2,1)}), bf16[16,8,8,896]{3,2,1,0:T(8,128)(2,1)}, u32[]{:S(2)}, u32[]{:S(2)}) async-start(bf16[16,8,8,896]{3,2,1,0:T(8,128)(2,1)} %bitcast.10), calls=%async_computation.2 | async-start | bytes 3670016 | tf_op jit(solution)/shard_map/all_to_all | solution.py:33
  114.7 2.0 %copy-done.1 = bf16[896,2048]{1,0:T(8,128)(2,1)S(1)} copy-done((bf16[896,2048]{1,0:T(8,128)(2,1)S(1)}, bf16[896,2048]{1,0:T(8,128)(2,1)}, u32[]{:S(2)}) %copy-start.1) | copy-done | bytes 3670040
  116.7 1.6 copy-done.5
  118.3 15.6 %mix.1 = (bf16[256,2048]{1,0:T(8,128)(2,1)}, bf16[64,2048]{1,0:T(8,128)(2,1)S(1)}) custom-call(s32[4]{0:T(128)S(1)} %compare_convert_fusion.valid_ref, bf16[16,4,16,896]{3,2,1,0:T(8,128)(2,1)S(1)} %bitcast.7, bf16[4,256,1024]{2,1,0:T(8,128)(2,1)S(1)} %copy-done.5, bf16[896,2048]{1,0:T(8,128)(2,1)S(1)} %copy-done.1), custom_call_target="tpu_custom_call" | custom-call | tf_op jit(solution)/shard_map/mix/pallas_call | solution.py:381
  133.9 9.1 %all-to-all-done.2.refs_1_ = bf16[16,8,8,896]{3,2,1,0:T(8,128)(2,1)} async-done(((bf16[16,8,8,896]{3,2,1,0:T(8,128)(2,1)}), bf16[16,8,8,896]{3,2,1,0:T(8,128)(2,1)}, u32[]{:S(2)}, u32[]{:S(2)}) %all-to-all-start.2) | async-done | bytes 1835040 | tf_op jit(solution)/shard_map/all_to_all | solution.py:33
  143.0 3.5 %reorder_back.1 = bf16[16,8,8,896]{3,2,1,0:T(8,128)(2,1)} custom-call(s32[128]{0:T(128)S(1)} %reshape.25.refs_0_, bf16[16,8,8,896]{3,2,1,0:T(8,128)(2,1)} %all-to-all-done.2.refs_1_), custom_call_target="tpu_custom_call" | custom-call | tf_op jit(solution)/shard_map/reorder_back/pallas_call | solution.py:123
  146.5 3.7 %all-to-all-start.3 = ((bf16[16,8,8,896]{3,2,1,0:T(8,128)(2,1)}), bf16[16,8,8,896]{3,2,1,0:T(8,128)(2,1)S(1)}, u32[]{:S(2)}, u32[]{:S(2)}) async-start(bf16[16,8,8,896]{3,2,1,0:T(8,128)(2,1)} %reorder_back.1), calls=%async_computation.3 | async-start | bytes 3670016 | tf_op jit(solution)/shard_map/all_to_all | solution.py:33
  150.2 3.1 %collective-permute-start.1 = (bf16[64,2048]{1,0:T(8,128)(2,1)S(1)}, bf16[64,2048]{1,0:T(8,128)(2,1)S(1)}, u32[]{:S(2)}, u32[]{:S(2)}) collective-permute-start(bf16[64,2048]{1,0:T(8,128)(2,1)S(1)} %get-tuple-element.30), channel_id=1, source_target_pairs={{0,1},{1,2},{2,3},{3,4},{4,5},{5,6},{6,7},{7,8},{8,9},{9,10},{10,1... | collective-permute-start | bytes 786440 | tf_op jit(solution)/shard_map/ppermute | solution.py:29
  153.3 29.3 %collective-permute-done.1.carried_ref = bf16[64,2048]{1,0:T(8,128)(2,1)S(1)} collective-permute-done((bf16[64,2048]{1,0:T(8,128)(2,1)S(1)}, bf16[64,2048]{1,0:T(8,128)(2,1)S(1)}, u32[]{:S(2)}, u32[]{:S(2)}) %collective-permute-start.1) | collective-permute-done | bytes 262176 | tf_op jit(solution)/shard_map/ppermute | solution.py:29
  182.7 1.7 join.1
  184.4 1.3 regroup.1
  (20 shorter events, 1.9 us)
Async XLA Ops:
  0.6 0.7 copy-start.6
  1.3 12.5 %copy-start.8 = (s32[4,2]{0,1:T(2,128)S(1)}, s32[4,2]{0,1:T(2,128)}, u32[]{:S(2)}) copy-start(s32[4,2]{0,1:T(2,128)} %param.13) | copy-start | bytes 100
  4.5 20.1 %collective-permute-start = (bf16[2,64,2048]{2,1,0:T(8,128)(2,1)S(1)}, bf16[2,64,2048]{2,1,0:T(8,128)(2,1)}, u32[]{:S(2)}, u32[]{:S(2)}) collective-permute-start(bf16[2,64,2048]{2,1,0:T(8,128)(2,1)S(1)} %get-tuple-element.19), channel_id=1, source_target_pairs={{1,0},{2,1},{3,2},{4,3},{5,4},{6,5},{7,6},{8,7},{9,8},{10,9},{11,1... | collective-permute-start | bytes 1572872 | tf_op jit(solution)/shard_map/ppermute | solution.py:29
  24.6 8.4 %copy-start.7 = (s32[4]{0:T(128)S(1)}, s32[4]{0:T(128)}, u32[]{:S(2)}) copy-start(s32[4]{0:T(128)} %label_ref.1) | copy-start | bytes 52
  24.6 10.4 %copy-start.2 = (bf16[256,2048]{1,0:T(8,128)(2,1)S(1)}, bf16[256,2048]{1,0:T(8,128)(2,1)}, u32[]{:S(2)}) copy-start(bf16[256,2048]{1,0:T(8,128)(2,1)} %q_ref.3) | copy-start | bytes 3145732
  24.6 38.8 %all-to-all-start = ((bf16[16,9,8,896]{3,2,1,0:T(8,128)(2,1)}), bf16[16,9,8,896]{3,2,1,0:T(8,128)(2,1)S(1)}, u32[]{:S(2)}, u32[]{:S(2)}) async-start(bf16[16,9,8,896]{3,2,1,0:T(8,128)(2,1)} %encode.1), calls=%async_computation | async-start | bytes 4128768 | tf_op jit(solution)/shard_map/all_to_all | solution.py:33
  35.0 2.0 %copy-start = (bf16[896,2048]{1,0:T(8,128)(2,1)S(1)}, bf16[896,2048]{1,0:T(8,128)(2,1)}, u32[]{:S(2)}) copy-start(bf16[896,2048]{1,0:T(8,128)(2,1)} %wv_ref.3) | copy-start | bytes 11010052
  37.0 1.2 copy-start.3
  38.3 2.0 %copy-start.4 = (bf16[896,2048]{1,0:T(8,128)(2,1)S(1)}, bf16[896,2048]{1,0:T(8,128)(2,1)}, u32[]{:S(2)}) copy-start(bf16[896,2048]{1,0:T(8,128)(2,1)} %wk_ref.1) | copy-start | bytes 11010052
  110.0 33.0 %all-to-all-start.2 = ((bf16[16,8,8,896]{3,2,1,0:T(8,128)(2,1)}), bf16[16,8,8,896]{3,2,1,0:T(8,128)(2,1)}, u32[]{:S(2)}, u32[]{:S(2)}) async-start(bf16[16,8,8,896]{3,2,1,0:T(8,128)(2,1)} %bitcast.10), calls=%async_computation.2 | async-start | bytes 3670016 | tf_op jit(solution)/shard_map/all_to_all | solution.py:33
  114.7 2.0 %copy-start.1 = (bf16[896,2048]{1,0:T(8,128)(2,1)S(1)}, bf16[896,2048]{1,0:T(8,128)(2,1)}, u32[]{:S(2)}) copy-start(bf16[896,2048]{1,0:T(8,128)(2,1)} %wv_ref.3) | copy-start | bytes 11010052
  116.7 1.6 copy-start.5
  146.5 37.9 %all-to-all-start.3 = ((bf16[16,8,8,896]{3,2,1,0:T(8,128)(2,1)}), bf16[16,8,8,896]{3,2,1,0:T(8,128)(2,1)S(1)}, u32[]{:S(2)}, u32[]{:S(2)}) async-start(bf16[16,8,8,896]{3,2,1,0:T(8,128)(2,1)} %reorder_back.1), calls=%async_computation.3 | async-start | bytes 3670016 | tf_op jit(solution)/shard_map/all_to_all | solution.py:33
  150.2 32.5 %collective-permute-start.1 = (bf16[64,2048]{1,0:T(8,128)(2,1)S(1)}, bf16[64,2048]{1,0:T(8,128)(2,1)S(1)}, u32[]{:S(2)}, u32[]{:S(2)}) collective-permute-start(bf16[64,2048]{1,0:T(8,128)(2,1)S(1)} %get-tuple-element.30), channel_id=1, source_target_pairs={{0,1},{1,2},{2,3},{3,4},{4,5},{5,6},{6,7},{7,8},{8,9},{9,10},{10,1... | collective-permute-start | bytes 786440 | tf_op jit(solution)/shard_map/ppermute | solution.py:29
